TPU v7x, 256 devices: a whole 4x4x8 slice. The times are simulated.
256 devices in a mesh: row: 8 (over z), col: 8 (over x, core), sub: 4 (over y).
Axes of the slice: x: 4, y: 4, z: 8, core: 2. Of those that a mesh axis runs over, the one named last changes fastest.
Arguments:
- front_entries: float32 [8192, 8192], P('row', ('col', 'sub')), may hold values from -1 to 4, as said below
- child_blocks: float32 [4, 2048, 2048], P('sub', 'row', 'col'), may hold values from -1 to 2, as said below
- child_map: int32 [4, 16], P('sub'), may hold values from 0 to 63, as said below
Outputs:
- factored: float32 [8192, 8192], P('row', ('col', 'sub'))
Inputs may be any that keep to these rules, and one draw needn't show every extreme that they name: Each row of child_map lists 16 different parent blocks in increasing order and ends with block 63. In natural order front_entries is a symmetric matrix, and the assembled front is positive definite. `child_blocks`: in natural order each child's contribution block is a symmetric matrix.
All inputs are finite; a program needn't handle non-finite values.
Results may differ from a plain program's by a relative error of at most 0.00005.
Values sent between devices are 32-bit elements; how exact they have to be, the bound alone decides.
A program may use at most 128 MiB of HBM per device.

v0:
```python
import jax
import jax.numpy as jnp
from jax import lax
from jax.sharding import PartitionSpec as P

BLK = 128
NPIV = 6
highest = lax.Precision.HIGHEST


def broadcast(value, axis, source):
    kept = jnp.where(lax.axis_index(axis) == source, value, 0).astype(value.dtype)
    return lax.psum(kept, axis)


def lookup(index_table, wanted):
    positions = jnp.arange(index_table.shape[0], dtype=jnp.int32)
    return jnp.sum(jnp.where(wanted[..., None] == positions, index_table, 0), axis=-1)


def body(front_entries, child_blocks, child_map):
    row_count = lax.axis_size("row")
    col_count = lax.axis_size("col")
    sub_count = lax.axis_size("sub")
    row_index = lax.axis_index("row")
    col_index = lax.axis_index("col")
    sub_index = lax.axis_index("sub")
    child_tile = child_blocks[0]
    mapping = child_map[0]
    local_rows = front_entries.shape[0]
    row_blocks = local_rows // BLK
    slot_count = front_entries.shape[1] // BLK
    col_blocks = slot_count * sub_count
    child_rows = child_tile.shape[0] // BLK
    child_cols = child_tile.shape[1] // BLK
    zero_carry = jnp.zeros((row_blocks, BLK, col_blocks, BLK), jnp.float32)
    incoming = lax.all_gather(child_tile[None], ("row", "col"), axis=0, tiled=True)
    piece_count = incoming.shape[0]
    source = jnp.arange(piece_count, dtype=jnp.int32)
    source_row = source // col_count
    source_col = source % col_count
    row_parent = lookup(
        mapping, jnp.arange(child_rows, dtype=jnp.int32)[None, :] * row_count + source_row[:, None]
    )
    col_parent = lookup(
        mapping, jnp.arange(child_cols, dtype=jnp.int32)[None, :] * col_count + source_col[:, None]
    )
    row_target = jnp.where(row_parent % row_count == row_index, row_parent // row_count, row_blocks)
    col_target = jnp.where(col_parent % col_count == col_index, col_parent // col_count, col_blocks)
    tile_stack = incoming.reshape(piece_count, child_rows, BLK, child_cols, BLK).transpose(
        0, 1, 3, 2, 4
    )
    spread_sum = zero_carry.at[row_target[:, :, None], :, col_target[:, None, :], :].add(
        tile_stack, mode="drop"
    )
    spread_sum = spread_sum.reshape(local_rows, col_blocks * BLK)
    summed = lax.psum_scatter(spread_sum, "sub", scatter_dimension=1, tiled=True)
    matrix = front_entries + summed
    row_global = jnp.repeat(jnp.arange(row_blocks, dtype=jnp.int32) * row_count + row_index, BLK)
    col_global = jnp.repeat(
        (sub_index * slot_count + jnp.arange(slot_count, dtype=jnp.int32)) * col_count + col_index,
        BLK,
    )
    for pivot_step in range(NPIV):
        sources_col_slot = pivot_step // col_count % slot_count
        sources_pivot_block = pivot_step // row_count
        col_source = matrix[:, sources_col_slot * BLK : (sources_col_slot + 1) * BLK]
        row_source = matrix[sources_pivot_block * BLK : (sources_pivot_block + 1) * BLK, :]
        root_group = pivot_step % col_count * sub_count + pivot_step // col_count // slot_count
        share_col_panel = broadcast(col_source, ("col", "sub"), root_group)
        pivot_block = pivot_step // row_count
        share_diagonal = share_col_panel[pivot_block * BLK : (pivot_block + 1) * BLK, :]
        share_pivot_row_panel, share_diagonal = (
            broadcast(row_source, "row", pivot_step % row_count),
            broadcast(share_diagonal, "row", pivot_step % row_count),
        )
        pivot_factor = jnp.linalg.cholesky(share_diagonal)
        lower_rows = jax.scipy.linalg.solve_triangular(
            pivot_factor, share_col_panel.T, lower=True
        ).T
        upper_rows = jax.scipy.linalg.solve_triangular(
            pivot_factor, share_pivot_row_panel, lower=True
        )
        left_factor = jnp.where(row_global[:, None] > pivot_step, lower_rows, 0.0)
        right_factor = jnp.where(col_global[None, :] > pivot_step, upper_rows, 0.0)
        factor_column = jnp.where(row_global[:, None] >= pivot_step, lower_rows, 0.0)
        left_factor, right_factor, column = (left_factor, right_factor, factor_column)
        matrix = matrix - jnp.dot(left_factor, right_factor, precision=highest)
        col_slot = pivot_step // col_count % slot_count
        is_owner = (col_index == pivot_step % col_count) & (
            sub_index == pivot_step // col_count // slot_count
        )
        existing = matrix[:, col_slot * BLK : (col_slot + 1) * BLK]
        matrix = matrix.at[:, col_slot * BLK : (col_slot + 1) * BLK].set(
            jnp.where(is_owner, column, existing)
        )
    upper_right = (row_global[:, None] < NPIV) & (col_global[None, :] >= NPIV)
    return jnp.where(upper_right, 0.0, matrix)


def solution(mesh):
    placed = (P("row", ("col", "sub")), P("sub", "row", "col"), P("sub", None))
    return jax.shard_map(
        body, mesh=mesh, in_specs=placed, out_specs=P("row", ("col", "sub")), check_vma=False
    )
```

profile of v0, /device:TPU:2, one launch (start us, length us, event | category | flops | bytes accessed | tf_op | source)
XLA Modules:
  0.0 1576.2 jit_solution(9138514772814132844)
XLA Ops:
  9.0 102.0 %all-gather.2.cloned.1.call-done = f32[64,256,256]{2,1,0:T(8,128)} async-done(((f32[1,256,256]{2,1,0:T(8,128)}), f32[64,256,256]{2,1,0:T(8,128)}) %all-gather.2.cloned.1.call-update) | async-done | bytes 16777232 | tf_op jit(solution)/shard_map/all_gather | solution.py:37
  111.0 20.8 %reshape.466 = f32[64,2,128,2,128]{4,3,2,1,0:T(2,128)} reshape(f32[64,256,256]{2,1,0:T(8,128)} %all-gather.2.cloned.1.call-done) | data formatting | bytes 33554432 | tf_op jit(solution)/shard_map/reshape | solution.py:50
  131.8 12.6 copy.62
  144.5 2.4 broadcast_in_dim.231
  146.9 49.3 %scatter_fusion = f32[8,128,8,128]{3,1,2,0:T(8,128)} fusion(f32[8,128,8,128]{3,1,2,0:T(8,128)} %broadcast_in_dim.231, s32[256]{0:T(256)S(1)} %reshape.468, f32[256,128,128]{2,1,0:T(8,128)} %bitcast.192), kind=kCustom, calls=%fused_computation | custom fusion | flops 4194304 | bytes 50333696 | tf_op jit(solution)/shard_map/scatter-add | solution.py:53
  196.2 5.5 copy.63
  201.7 5.2 copy.98
  208.1 48.3 %reduce-scatter.2.cloned.1.call-done = f32[1024,256]{0,1:T(8,128)} async-done(((f32[1024,1024]{0,1:T(8,128)}), f32[1024,256]{0,1:T(8,128)}) %reduce-scatter.2.cloned.1.call-update) | async-done | bytes 1048592 | tf_op jit(solution)/shard_map/reduce_scatter | solution.py:57
  260.1 113.2 %all-reduce.19.cloned.1.call-done = f32[1024,128]{0,1:T(8,128)} async-done(((f32[1024,128]{0,1:T(8,128)}), f32[1024,128]{0,1:T(8,128)}) %all-reduce.19.cloned.1.call-update) | async-done | bytes 524304 | tf_op jit(solution)/shard_map/psum | solution.py:13
  373.3 1.5 slice_select_fusion.12
  375.1 73.6 %all-reduce.41.cloned.1.call-done = (f32[128,256]{0,1:T(8,128)}, f32[128,128]{0,1:T(8,128)}) async-done(((f32[128,256]{0,1:T(8,128)}, f32[128,128]{0,1:T(8,128)}), (f32[128,256]{0,1:T(8,128)}, f32[128,128]{0,1:T(8,128)})) %all-reduce.41.cloned.1.call-update) | async-done | bytes 196624 | tf_op jit(solution)/shard_map/psum | solution.py:13
  450.4 11.7 cholesky.104
  463.5 9.8 custom-call.20
  474.5 1.7 fusion.11
  477.2 1.6 broadcast_select_fusion.4
  479.6 111.7 %all-reduce.21.cloned.1.call-done = f32[1024,128]{0,1:T(8,128)} async-done(((f32[1024,128]{0,1:T(8,128)}), f32[1024,128]{0,1:T(8,128)}) %all-reduce.21.cloned.1.call-update) | async-done | bytes 524304 | tf_op jit(solution)/shard_map/psum | solution.py:13
  591.2 1.5 slice_select_fusion.11
  593.1 73.5 %all-reduce.39.cloned.1.call-done = (f32[128,256]{0,1:T(8,128)}, f32[128,128]{0,1:T(8,128)}) async-done(((f32[128,256]{0,1:T(8,128)}, f32[128,128]{0,1:T(8,128)}), (f32[128,256]{0,1:T(8,128)}, f32[128,128]{0,1:T(8,128)})) %all-reduce.39.cloned.1.call-update) | async-done | bytes 196624 | tf_op jit(solution)/shard_map/psum | solution.py:13
  668.4 11.7 cholesky.115
  681.5 9.8 custom-call.22
  692.4 1.7 fusion.9
  695.1 1.6 broadcast_select_fusion.3
  697.5 111.7 %all-reduce.23.cloned.1.call-done = f32[1024,128]{0,1:T(8,128)} async-done(((f32[1024,128]{0,1:T(8,128)}), f32[1024,128]{0,1:T(8,128)}) %all-reduce.23.cloned.1.call-update) | async-done | bytes 524304 | tf_op jit(solution)/shard_map/psum | solution.py:13
  809.2 1.5 slice_select_fusion.10
  811.1 73.6 %all-reduce.37.cloned.1.call-done = (f32[128,256]{0,1:T(8,128)}, f32[128,128]{0,1:T(8,128)}) async-done(((f32[128,256]{0,1:T(8,128)}, f32[128,128]{0,1:T(8,128)}), (f32[128,256]{0,1:T(8,128)}, f32[128,128]{0,1:T(8,128)})) %all-reduce.37.cloned.1.call-update) | async-done | bytes 196624 | tf_op jit(solution)/shard_map/psum | solution.py:13
  886.5 11.7 cholesky.126
  899.6 9.8 custom-call.24
  910.6 1.7 fusion.7
  913.3 1.6 broadcast_select_fusion.2
  915.7 111.7 %all-reduce.25.cloned.1.call-done = f32[1024,128]{0,1:T(8,128)} async-done(((f32[1024,128]{0,1:T(8,128)}), f32[1024,128]{0,1:T(8,128)}) %all-reduce.25.cloned.1.call-update) | async-done | bytes 524304 | tf_op jit(solution)/shard_map/psum | solution.py:13
  1027.3 1.5 slice_select_fusion.9
  1029.4 73.3 %all-reduce.35.cloned.1.call-done = (f32[128,256]{0,1:T(8,128)}, f32[128,128]{0,1:T(8,128)}) async-done(((f32[128,256]{0,1:T(8,128)}, f32[128,128]{0,1:T(8,128)}), (f32[128,256]{0,1:T(8,128)}, f32[128,128]{0,1:T(8,128)})) %all-reduce.35.cloned.1.call-update) | async-done | bytes 196624 | tf_op jit(solution)/shard_map/psum | solution.py:13
  1104.5 11.7 cholesky.137
  1117.6 9.8 custom-call.26
  1128.5 1.7 fusion.5
  1131.2 1.6 broadcast_select_fusion.1
  1133.7 111.7 %all-reduce.27.cloned.1.call-done = f32[1024,128]{0,1:T(8,128)} async-done(((f32[1024,128]{0,1:T(8,128)}), f32[1024,128]{0,1:T(8,128)}) %all-reduce.27.cloned.1.call-update) | async-done | bytes 524304 | tf_op jit(solution)/shard_map/psum | solution.py:13
  1245.3 1.5 slice_select_fusion.8
  1247.1 73.6 %all-reduce.33.cloned.1.call-done = (f32[128,256]{0,1:T(8,128)}, f32[128,128]{0,1:T(8,128)}) async-done(((f32[128,256]{0,1:T(8,128)}, f32[128,128]{0,1:T(8,128)}), (f32[128,256]{0,1:T(8,128)}, f32[128,128]{0,1:T(8,128)})) %all-reduce.33.cloned.1.call-update) | async-done | bytes 196624 | tf_op jit(solution)/shard_map/psum | solution.py:13
  1322.5 11.7 cholesky.148
  1335.5 9.8 custom-call.28
  1346.5 1.7 fusion.3
  1349.2 1.6 broadcast_select_fusion
  1351.8 111.5 %all-reduce.29.cloned.1.call-done = f32[1024,128]{0,1:T(8,128)} async-done(((f32[1024,128]{0,1:T(8,128)}), f32[1024,128]{0,1:T(8,128)}) %all-reduce.29.cloned.1.call-update) | async-done | bytes 524304 | tf_op jit(solution)/shard_map/psum | solution.py:13
  1464.9 73.8 %all-reduce.31.cloned.1.call-done = (f32[128,256]{0,1:T(8,128)}, f32[128,128]{0,1:T(8,128)}) async-done(((f32[128,256]{0,1:T(8,128)}, f32[128,128]{0,1:T(8,128)}), (f32[128,256]{0,1:T(8,128)}, f32[128,128]{0,1:T(8,128)})) %all-reduce.31.cloned.1.call-update) | async-done | bytes 196624 | tf_op jit(solution)/shard_map/psum | solution.py:13
  1540.5 11.7 cholesky.159
  1553.6 9.8 custom-call.30
  1564.5 1.7 fusion.1
  (133 shorter events, 48.8 us)
Async XLA Ops:
  6.5 104.5 %all-gather.2.cloned.1.call-start = ((), (), s32[]{:S(2)}) async-start(), calls=%async_computation.1 | async-start | bytes 17039360 | tf_op jit(solution)/shard_map/all_gather | solution.py:37
  7.3 249.2 %reduce-scatter.2.cloned.1.call-start = ((), (), s32[]{:S(2)}) async-start(), calls=%async_computation.2 | async-start | bytes 5242880 | tf_op jit(solution)/shard_map/reduce_scatter | solution.py:57
  196.2 10.7 copy-start
  206.9 166.4 %all-reduce.19.cloned.1.call-start = ((), (), s32[]{:S(2)}) async-start(), calls=%async_computation.3 | async-start | bytes 1048576 | tf_op jit(solution)/shard_map/psum | solution.py:13
  258.7 190.0 %all-reduce.41.cloned.1.call-start = ((), (), s32[]{:S(2)}) async-start(), calls=%async_computation.14 | async-start | bytes 393216 | tf_op jit(solution)/shard_map/psum | solution.py:13
  374.8 216.5 %all-reduce.21.cloned.1.call-start = ((), (), s32[]{:S(2)}) async-start(), calls=%async_computation.4 | async-start | bytes 1048576 | tf_op jit(solution)/shard_map/psum | solution.py:13
  478.8 187.8 %all-reduce.39.cloned.1.call-start = ((), (), s32[]{:S(2)}) async-start(), calls=%async_computation.13 | async-start | bytes 393216 | tf_op jit(solution)/shard_map/psum | solution.py:13
  592.7 216.5 %all-reduce.23.cloned.1.call-start = ((), (), s32[]{:S(2)}) async-start(), calls=%async_computation.5 | async-start | bytes 1048576 | tf_op jit(solution)/shard_map/psum | solution.py:13
  696.8 188.0 %all-reduce.37.cloned.1.call-start = ((), (), s32[]{:S(2)}) async-start(), calls=%async_computation.12 | async-start | bytes 393216 | tf_op jit(solution)/shard_map/psum | solution.py:13
  810.7 216.6 %all-reduce.25.cloned.1.call-start = ((), (), s32[]{:S(2)}) async-start(), calls=%async_computation.6 | async-start | bytes 1048576 | tf_op jit(solution)/shard_map/psum | solution.py:13
  914.9 187.8 %all-reduce.35.cloned.1.call-start = ((), (), s32[]{:S(2)}) async-start(), calls=%async_computation.11 | async-start | bytes 393216 | tf_op jit(solution)/shard_map/psum | solution.py:13
  1028.8 216.5 %all-reduce.27.cloned.1.call-start = ((), (), s32[]{:S(2)}) async-start(), calls=%async_computation.7 | async-start | bytes 1048576 | tf_op jit(solution)/shard_map/psum | solution.py:13
  1132.9 187.8 %all-reduce.33.cloned.1.call-start = ((), (), s32[]{:S(2)}) async-start(), calls=%async_computation.10 | async-start | bytes 393216 | tf_op jit(solution)/shard_map/psum | solution.py:13
  1246.8 216.5 %all-reduce.29.cloned.1.call-start = ((), (), s32[]{:S(2)}) async-start(), calls=%async_computation.8 | async-start | bytes 1048576 | tf_op jit(solution)/shard_map/psum | solution.py:13
  1350.8 187.9 %all-reduce.31.cloned.1.call-start = ((), (), s32[]{:S(2)}) async-start(), calls=%async_computation.9 | async-start | bytes 393216 | tf_op jit(solution)/shard_map/psum | solution.py:13
Sparse Core Ops, SparseCore 0:
  10.1 100.8 all-gather.1
  207.0 49.4 reduce-scatter.1
  259.6 113.5 all-reduce.18
  375.5 73.0 all-reduce.40
  478.9 112.2 all-reduce.20
  593.5 73.0 all-reduce.38
  696.9 112.2 all-reduce.22
  811.6 73.0 all-reduce.36
  915.0 112.2 all-reduce.24
  1029.6 73.0 all-reduce.34
  1133.0 112.2 all-reduce.26
  1247.5 73.0 all-reduce.32
  1351.0 112.3 all-reduce.28
  1465.6 73.0 all-reduce.30
where the time goes:
time: 1580 us
  waiting for transfers between devices  1260 us (80%)
  other arithmetic  217 us (14%)
  local copies, waits for them, and re-layouts  55.7 us (4%)
  matrix products  23.1 us (1%)
    psum x12, waiting for transfers between devices, broadcast(): return lax.psum(kept, axis)  1110 us
    all_gather x1, waiting for transfers between devices, body(): lax.all_gather(child_tile[None], ('row', 'col'), axis=0, tiled=True)  102 us
    another operation x18, other arithmetic, body(): pivot_factor = jnp.linalg.cholesky(share_diagonal)  74.3 us
    another operation x12, other arithmetic, body(): jax.scipy.linalg.solve_triangular(pivot_factor, share_col_panel.T, lower=...  62.8 us
    scatter-add x1, other arithmetic, body(): zero_carry.at[row_target[:, :, None], :, col_target[:, None, :], :]  49.3 us
    reduce_scatter x1, waiting for transfers between devices, body(): lax.psum_scatter(spread_sum, 'sub', scatter_dimension=1, tiled=True)  48.3 us
  transfers between devices with their start and end apart: 14, of which 14 were waited for; matrix products, arithmetic and copies ran while one was open for 1% of the time, Pallas kernels for 0%

commit v1 on v0

--- a/solution.py
+++ b/solution.py
@@ -10,7 +10,7 @@
 
 def broadcast(value, axis, source):
     kept = jnp.where(lax.axis_index(axis) == source, value, 0).astype(value.dtype)
-    return lax.psum(kept, axis)
+    return jnp.sum(lax.all_gather(kept, axis), axis=0)
 
 
 def lookup(index_table, wanted):

time: 1580 us -> 1460 us (0.924)
  waiting for transfers between devices: 1260 us -> 839 us
  blocking collectives: 0 us -> 163 us
  local copies, waits for them, and re-layouts: 55.7 us -> 166 us
  other arithmetic: 217 us -> 260 us
    psum x12 -> x0, waiting for transfers between devices: 1110 us -> none  [broadcast(): return lax.psum(kept, axis)]
    all_gather x0 -> x12, waiting for transfers between devices: none -> 684 us  [broadcast(): return jnp.sum(lax.all_gather(kept, axis), axis=0)]
    all_gather x0 -> x6, blocking collectives: none -> 163 us  [broadcast(): return jnp.sum(lax.all_gather(kept, axis), axis=0)]
    unnamed x4 -> x22, local copies, waits for them, and re-layouts: 5.5 us -> 121 us
    reduce_sum x0 -> x18, other arithmetic: none -> 56.3 us  [broadcast(): return jnp.sum(lax.all_gather(kept, axis), axis=0)]
where the time goes in v1:
time: 1460 us
  waiting for transfers between devices  839 us (57%)
  other arithmetic  260 us (18%)
  local copies, waits for them, and re-layouts  166 us (11%)
  blocking collectives  163 us (11%)
    all_gather x12, waiting for transfers between devices, broadcast(): return jnp.sum(lax.all_gather(kept, axis), axis=0)  684 us
    all_gather x6, blocking collectives, broadcast(): return jnp.sum(lax.all_gather(kept, axis), axis=0)  163 us
    unnamed x22, local copies, waits for them, and re-layouts  121 us
    all_gather x1, waiting for transfers between devices, body(): lax.all_gather(child_tile[None], ('row', 'col'), axis=0, tiled=True)  102 us
    another operation x18, other arithmetic, body(): pivot_factor = jnp.linalg.cholesky(share_diagonal)  74.3 us
    another operation x12, other arithmetic, body(): jax.scipy.linalg.solve_triangular(pivot_factor, share_col_panel.T, lower=...  62.8 us
    reduce_sum x18, other arithmetic, broadcast(): return jnp.sum(lax.all_gather(kept, axis), axis=0)  56.3 us
    scatter-add x1, other arithmetic, body(): zero_carry.at[row_target[:, :, None], :, col_target[:, None, :], :]  49.3 us
  transfers between devices with their start and end apart: 14, of which 14 were waited for; matrix products, arithmetic and copies ran while one was open for 1% of the time, Pallas kernels for 0%

profile of v1, /device:TPU:2, one launch (start us, length us, event | category | flops | bytes accessed | tf_op | source)
XLA Modules:
  0.0 1455.6 jit_solution(3601821902315125295)
XLA Ops:
  9.0 102.0 %all-gather.32.cloned.1.call-done = f32[64,256,256]{2,1,0:T(8,128)} async-done(((f32[1,256,256]{2,1,0:T(8,128)}), f32[64,256,256]{2,1,0:T(8,128)}) %all-gather.32.cloned.1.call-update) | async-done | bytes 16777232 | tf_op jit(solution)/shard_map/all_gather | solution.py:37
  111.0 20.8 %reshape.466 = f32[64,2,128,2,128]{4,3,2,1,0:T(2,128)} reshape(f32[64,256,256]{2,1,0:T(8,128)} %all-gather.32.cloned.1.call-done) | data formatting | bytes 33554432 | tf_op jit(solution)/shard_map/reshape | solution.py:50
  131.8 12.6 copy.62
  146.9 49.3 %scatter_fusion = f32[8,128,8,128]{3,1,2,0:T(8,128)} fusion(f32[8,128,8,128]{3,1,2,0:T(8,128)} %broadcast_in_dim.231, s32[256]{0:T(256)S(1)} %reshape.468, f32[256,128,128]{2,1,0:T(8,128)} %bitcast.282), kind=kCustom, calls=%fused_computation | custom fusion | flops 4194304 | bytes 50333696 | tf_op jit(solution)/shard_map/scatter-add | solution.py:53
  196.2 5.5 copy.63
  207.3 49.1 %reduce-scatter.2.cloned.1.call-done = f32[1024,256]{0,1:T(8,128)} async-done(((f32[1024,1024]{0,1:T(8,128)}), f32[1024,256]{0,1:T(8,128)}) %reduce-scatter.2.cloned.1.call-update) | async-done | bytes 1048592 | tf_op jit(solution)/shard_map/reduce_scatter | solution.py:57
  260.7 36.9 %all-gather.36.cloned.1.call-done = f32[1024,256]{0,1:T(8,128)} async-done(((f32[128,256]{0,1:T(8,128)}), f32[1024,256]{0,1:T(8,128)}) %all-gather.36.cloned.1.call-update) | async-done | bytes 1048592 | tf_op jit(solution)/shard_map/all_gather | solution.py:13
  299.3 77.4 %all-gather.34.cloned.1.call-done = f32[32768,128]{0,1:T(8,128)} async-done(((f32[1024,128]{0,1:T(8,128)}), f32[32768,128]{0,1:T(8,128)}) %all-gather.34.cloned.1.call-update) | async-done | bytes 16777232 | tf_op jit(solution)/shard_map/all_gather | solution.py:13
  376.7 17.7 %copy.97 = f32[16,8,32,1024]{3,2,1,0:T(8,128)} copy(f32[16,8,32,1024]{3,1,2,0:T(8,128)} %bitcast.284) | data formatting | bytes 33554432
  394.4 9.0 bitcast_reduce_fusion.5
  403.4 27.4 %all-gather.1 = f32[1024,128]{0,1:T(8,128)S(1)} all-gather(f32[128,128]{0,1:T(8,128)S(1)} %slice_select_fusion.12), channel_id=3, replica_groups=mesh['row'=8,'col'=8,'sub'=4] {'row'}, dimensions={0}, use_global_device_ids=true | all-gather | bytes 589824 | tf_op jit(solution)/shard_map/all_gather | solution.py:13
  431.2 11.7 cholesky.104
  444.2 9.8 custom-call.20
  459.4 36.6 %all-gather.40.cloned.1.call-done = f32[1024,256]{0,1:T(8,128)} async-done(((f32[128,256]{0,1:T(8,128)}), f32[1024,256]{0,1:T(8,128)}) %all-gather.40.cloned.1.call-update) | async-done | bytes 1048592 | tf_op jit(solution)/shard_map/all_gather | solution.py:13
  497.6 77.4 %all-gather.38.cloned.1.call-done = f32[32768,128]{0,1:T(8,128)} async-done(((f32[1024,128]{0,1:T(8,128)}), f32[32768,128]{0,1:T(8,128)}) %all-gather.38.cloned.1.call-update) | async-done | bytes 16777232 | tf_op jit(solution)/shard_map/all_gather | solution.py:13
  575.1 17.7 %copy.100 = f32[16,8,32,1024]{3,2,1,0:T(8,128)} copy(f32[16,8,32,1024]{3,1,2,0:T(8,128)} %bitcast.288) | data formatting | bytes 33554432
  592.8 9.0 bitcast_reduce_fusion.4
  601.8 27.1 %all-gather.4 = f32[1024,128]{0,1:T(8,128)S(1)} all-gather(f32[128,128]{0,1:T(8,128)S(1)} %slice_select_fusion.11), channel_id=6, replica_groups=mesh['row'=8,'col'=8,'sub'=4] {'row'}, dimensions={0}, use_global_device_ids=true | all-gather | bytes 589824 | tf_op jit(solution)/shard_map/all_gather | solution.py:13
  629.2 11.7 cholesky.115
  642.3 9.8 custom-call.22
  657.7 36.2 %all-gather.44.cloned.1.call-done = f32[1024,256]{0,1:T(8,128)} async-done(((f32[128,256]{0,1:T(8,128)}), f32[1024,256]{0,1:T(8,128)}) %all-gather.44.cloned.1.call-update) | async-done | bytes 1048592 | tf_op jit(solution)/shard_map/all_gather | solution.py:13
  695.6 77.6 %all-gather.42.cloned.1.call-done = f32[32768,128]{0,1:T(8,128)} async-done(((f32[1024,128]{0,1:T(8,128)}), f32[32768,128]{0,1:T(8,128)}) %all-gather.42.cloned.1.call-update) | async-done | bytes 16777232 | tf_op jit(solution)/shard_map/all_gather | solution.py:13
  773.2 17.7 %copy.103 = f32[16,8,32,1024]{3,2,1,0:T(8,128)} copy(f32[16,8,32,1024]{3,1,2,0:T(8,128)} %bitcast.286) | data formatting | bytes 33554432
  790.9 9.0 bitcast_reduce_fusion.3
  799.9 27.3 %all-gather.7 = f32[1024,128]{0,1:T(8,128)S(1)} all-gather(f32[128,128]{0,1:T(8,128)S(1)} %slice_select_fusion.10), channel_id=9, replica_groups=mesh['row'=8,'col'=8,'sub'=4] {'row'}, dimensions={0}, use_global_device_ids=true | all-gather | bytes 589824 | tf_op jit(solution)/shard_map/all_gather | solution.py:13
  827.6 11.7 cholesky.126
  840.6 9.8 custom-call.24
  855.7 36.6 %all-gather.48.cloned.1.call-done = f32[1024,256]{0,1:T(8,128)} async-done(((f32[128,256]{0,1:T(8,128)}), f32[1024,256]{0,1:T(8,128)}) %all-gather.48.cloned.1.call-update) | async-done | bytes 1048592 | tf_op jit(solution)/shard_map/all_gather | solution.py:13
  893.9 77.4 %all-gather.46.cloned.1.call-done = f32[32768,128]{0,1:T(8,128)} async-done(((f32[1024,128]{0,1:T(8,128)}), f32[32768,128]{0,1:T(8,128)}) %all-gather.46.cloned.1.call-update) | async-done | bytes 16777232 | tf_op jit(solution)/shard_map/all_gather | solution.py:13
  971.4 17.7 %copy.106 = f32[16,8,32,1024]{3,2,1,0:T(8,128)} copy(f32[16,8,32,1024]{3,1,2,0:T(8,128)} %bitcast.289) | data formatting | bytes 33554432
  989.1 9.0 bitcast_reduce_fusion.2
  998.1 27.1 %all-gather.10 = f32[1024,128]{0,1:T(8,128)S(1)} all-gather(f32[128,128]{0,1:T(8,128)S(1)} %slice_select_fusion.9), channel_id=12, replica_groups=mesh['row'=8,'col'=8,'sub'=4] {'row'}, dimensions={0}, use_global_device_ids=true | all-gather | bytes 589824 | tf_op jit(solution)/shard_map/all_gather | solution.py:13
  1025.5 11.7 cholesky.137
  1038.6 9.8 custom-call.26
  1053.8 36.4 %all-gather.52.cloned.1.call-done = f32[1024,256]{0,1:T(8,128)} async-done(((f32[128,256]{0,1:T(8,128)}), f32[1024,256]{0,1:T(8,128)}) %all-gather.52.cloned.1.call-update) | async-done | bytes 1048592 | tf_op jit(solution)/shard_map/all_gather | solution.py:13
  1091.9 77.4 %all-gather.50.cloned.1.call-done = f32[32768,128]{0,1:T(8,128)} async-done(((f32[1024,128]{0,1:T(8,128)}), f32[32768,128]{0,1:T(8,128)}) %all-gather.50.cloned.1.call-update) | async-done | bytes 16777232 | tf_op jit(solution)/shard_map/all_gather | solution.py:13
  1169.3 17.7 %copy.109 = f32[16,8,32,1024]{3,2,1,0:T(8,128)} copy(f32[16,8,32,1024]{3,1,2,0:T(8,128)} %bitcast.285) | data formatting | bytes 33554432
  1187.0 9.0 bitcast_reduce_fusion.1
  1196.1 27.3 %all-gather.13 = f32[1024,128]{0,1:T(8,128)S(1)} all-gather(f32[128,128]{0,1:T(8,128)S(1)} %slice_select_fusion.8), channel_id=15, replica_groups=mesh['row'=8,'col'=8,'sub'=4] {'row'}, dimensions={0}, use_global_device_ids=true | all-gather | bytes 589824 | tf_op jit(solution)/shard_map/all_gather | solution.py:13
  1223.7 11.7 cholesky.148
  1236.8 9.8 custom-call.28
  1251.8 36.6 %all-gather.56.cloned.1.call-done = f32[1024,256]{0,1:T(8,128)} async-done(((f32[128,256]{0,1:T(8,128)}), f32[1024,256]{0,1:T(8,128)}) %all-gather.56.cloned.1.call-update) | async-done | bytes 1048592 | tf_op jit(solution)/shard_map/all_gather | solution.py:13
  1290.1 77.4 %all-gather.54.cloned.1.call-done = f32[32768,128]{0,1:T(8,128)} async-done(((f32[1024,128]{0,1:T(8,128)}), f32[32768,128]{0,1:T(8,128)}) %all-gather.54.cloned.1.call-update) | async-done | bytes 16777232 | tf_op jit(solution)/shard_map/all_gather | solution.py:13
  1367.6 17.7 %copy.112 = f32[16,8,32,1024]{3,2,1,0:T(8,128)} copy(f32[16,8,32,1024]{3,1,2,0:T(8,128)} %bitcast.287) | data formatting | bytes 33554432
  1385.3 9.0 bitcast_reduce_fusion
  1394.3 27.1 %all-gather.16 = f32[1024,128]{0,1:T(8,128)S(1)} all-gather(f32[128,128]{0,1:T(8,128)S(1)} %slice_select_fusion.7), channel_id=18, replica_groups=mesh['row'=8,'col'=8,'sub'=4] {'row'}, dimensions={0}, use_global_device_ids=true | all-gather | bytes 589824 | tf_op jit(solution)/shard_map/all_gather | solution.py:13
  1421.7 11.7 cholesky.159
  1434.8 9.8 custom-call.30
  (169 shorter events, 65.3 us)
Async XLA Ops:
  6.5 104.5 %all-gather.32.cloned.1.call-start = ((), (), s32[]{:S(2)}) async-start(), calls=%async_computation.1 | async-start | bytes 17039360 | tf_op jit(solution)/shard_map/all_gather | solution.py:37
  7.3 249.1 %reduce-scatter.2.cloned.1.call-start = ((), (), s32[]{:S(2)}) async-start(), calls=%async_computation.2 | async-start | bytes 5242880 | tf_op jit(solution)/shard_map/reduce_scatter | solution.py:57
  196.2 10.7 copy-start
  206.9 90.7 %all-gather.36.cloned.1.call-start = ((), (), s32[]{:S(2)}) async-start(), calls=%async_computation.4 | async-start | bytes 1179648 | tf_op jit(solution)/shard_map/all_gather | solution.py:13
  258.4 118.3 %all-gather.34.cloned.1.call-start = ((), (), s32[]{:S(2)}) async-start(), calls=%async_computation.3 | async-start | bytes 17301504 | tf_op jit(solution)/shard_map/all_gather | solution.py:13
  259.4 236.6 %all-gather.40.cloned.1.call-start = ((), (), s32[]{:S(2)}) async-start(), calls=%async_computation.6 | async-start | bytes 1179648 | tf_op jit(solution)/shard_map/all_gather | solution.py:13
  458.3 116.7 %all-gather.38.cloned.1.call-start = ((), (), s32[]{:S(2)}) async-start(), calls=%async_computation.5 | async-start | bytes 17301504 | tf_op jit(solution)/shard_map/all_gather | solution.py:13
  458.9 235.0 %all-gather.44.cloned.1.call-start = ((), (), s32[]{:S(2)}) async-start(), calls=%async_computation.8 | async-start | bytes 1179648 | tf_op jit(solution)/shard_map/all_gather | solution.py:13
  656.4 116.8 %all-gather.42.cloned.1.call-start = ((), (), s32[]{:S(2)}) async-start(), calls=%async_computation.7 | async-start | bytes 17301504 | tf_op jit(solution)/shard_map/all_gather | solution.py:13
  657.1 235.2 %all-gather.48.cloned.1.call-start = ((), (), s32[]{:S(2)}) async-start(), calls=%async_computation.10 | async-start | bytes 1179648 | tf_op jit(solution)/shard_map/all_gather | solution.py:13
  854.7 116.7 %all-gather.46.cloned.1.call-start = ((), (), s32[]{:S(2)}) async-start(), calls=%async_computation.9 | async-start | bytes 17301504 | tf_op jit(solution)/shard_map/all_gather | solution.py:13
  855.3 234.9 %all-gather.52.cloned.1.call-start = ((), (), s32[]{:S(2)}) async-start(), calls=%async_computation.12 | async-start | bytes 1179648 | tf_op jit(solution)/shard_map/all_gather | solution.py:13
  1052.7 116.7 %all-gather.50.cloned.1.call-start = ((), (), s32[]{:S(2)}) async-start(), calls=%async_computation.11 | async-start | bytes 17301504 | tf_op jit(solution)/shard_map/all_gather | solution.py:13
  1053.2 235.2 %all-gather.56.cloned.1.call-start = ((), (), s32[]{:S(2)}) async-start(), calls=%async_computation.14 | async-start | bytes 1179648 | tf_op jit(solution)/shard_map/all_gather | solution.py:13
  1250.9 116.7 %all-gather.54.cloned.1.call-start = ((), (), s32[]{:S(2)}) async-start(), calls=%async_computation.13 | async-start | bytes 17301504 | tf_op jit(solution)/shard_map/all_gather | solution.py:13
Sparse Core Ops, SparseCore 0:
  10.1 100.8 all-gather.31
  207.0 49.3 reduce-scatter.1
  258.6 39.0 all-gather.35
  300.1 76.5 all-gather.33
  458.4 37.4 all-gather.39
  498.4 76.5 all-gather.37
  656.5 37.3 all-gather.43
  696.5 76.5 all-gather.41
  854.8 37.3 all-gather.47
  894.7 76.5 all-gather.45
  1052.8 37.3 all-gather.51
  1092.7 76.5 all-gather.49
  1251.0 37.3 all-gather.55
  1290.9 76.5 all-gather.53
